TPU v7x, 32 devices: a whole 2x2x4 slice. The times are simulated.
32 devices in a mesh: expert: 4 (over y, x), shard: 8 (over z, core).
Axes of the slice: x: 2, y: 2, z: 4, core: 2. Of those that a mesh axis runs over, the one named last changes fastest.
Arguments:
- hidden: bfloat16 [64, 4096], P('shard'), may hold values from -6 to 6
- queries: bfloat16 [64, 32, 128], P('shard', 'expert'), may hold values from -30 to 30
- key_cache: bfloat16 [64, 512, 8, 128], P('shard', None, 'expert'), may hold values from -16 to 16
- value_cache: bfloat16 [64, 512, 8, 128], P('shard', None, 'expert'), may hold values from -6 to 6
- out_weight: bfloat16 [4096, 4096], P('expert', 'shard'), may hold values from -0.09375 to 0.09375
- norm_gain: bfloat16 [4096], replicated, may hold values from 0.099609375 to 1.8984375
- router: bfloat16 [4096, 8], replicated, may hold values from -0.09375 to 0.09375
- expert_ids: int32 [64, 2], replicated, may hold values from 0 to 7, all different within a row; in each aligned block of 64 rows (0 to 63, 64 to 127, ...) at most 32 rows name the same one
- gate_weight: bfloat16 [8, 4096, 14336], P('expert', None, 'shard'), may hold values from -0.09375 to 0.09375
- up_weight: bfloat16 [8, 4096, 14336], P('expert', None, 'shard'), may hold values from -0.09375 to 0.09375
- down_weight: bfloat16 [8, 14336, 4096], P('expert', 'shard'), may hold values from -0.046875 to 0.046875
Outputs:
- layer_out: bfloat16 [64, 4096], P('shard')
Inputs may be any that keep to these rules, and one draw needn't show every extreme that they name: `expert_ids`: each token names two different experts; over all 64 tokens no expert is named by more than 32 tokens, a bound that some block reaches.
All inputs are finite; a program needn't handle non-finite values.
Results may differ from a plain program's by a relative error of at most 0.008.
Values may be sent and summed in bfloat16 or wider, within the bound.
A program may use at most 128 MiB of HBM per device.

v0:
```python
import math

import jax
import jax.numpy as jnp
from jax import lax
from jax.sharding import PartitionSpec as P


def on_device(
    hidden,
    queries,
    key_cache,
    value_cache,
    out_weight,
    norm_gain,
    router,
    expert_ids,
    gate_weight,
    up_weight,
    down_weight,
):
    count_local, heads_local, head_size = queries.shape
    kv_local = key_cache.shape[2]
    per_kv = heads_local // kv_local
    query_blocks = queries.reshape(count_local, kv_local, per_kv, head_size)
    scores = jnp.einsum(
        "tkgd,tpkd->tkgp", query_blocks, key_cache, preferred_element_type=jnp.float32
    ) / math.sqrt(head_size)
    attn_weights = jax.nn.softmax(scores, axis=-1).astype(jnp.bfloat16)
    attended = jnp.einsum(
        "tkgp,tpkd->tkgd", attn_weights, value_cache, preferred_element_type=jnp.float32
    )
    attended = attended.astype(jnp.bfloat16).reshape(count_local, heads_local * head_size)
    all_attended = lax.all_gather(attended, "shard", axis=0, tiled=True)
    partial_cols = jnp.dot(all_attended, out_weight, preferred_element_type=jnp.float32)
    partial_heads = lax.all_to_all(partial_cols, "shard", split_axis=0, concat_axis=1, tiled=True)
    attn_out = lax.psum(partial_heads, "expert")
    stream = hidden.astype(jnp.float32) + attn_out
    scaled = stream * lax.rsqrt(jnp.mean(stream * stream, axis=-1, keepdims=True) + 1e-05)
    normed = (scaled * norm_gain.astype(jnp.float32)).astype(jnp.bfloat16)
    everyone = lax.all_gather(normed, "shard", axis=0, tiled=True)
    token_count = everyone.shape[0]
    logits = jnp.dot(everyone, router, preferred_element_type=jnp.float32)
    top_first = jnp.take_along_axis(logits, expert_ids[:, 0:1], axis=1)[:, 0]
    top_second = jnp.take_along_axis(logits, expert_ids[:, 1:2], axis=1)[:, 0]
    weight_first = 1.0 / (1.0 + jnp.exp(top_second - top_first))
    weight_second = 1.0 / (1.0 + jnp.exp(top_first - top_second))
    local_experts = gate_weight.shape[0]
    group_index = lax.axis_index("expert")
    summed = jnp.zeros((token_count, everyone.shape[1]), jnp.float32)
    for member in range(local_experts):
        expert = group_index * local_experts + member
        in_first = expert_ids[:, 0] == expert
        in_second = expert_ids[:, 1] == expert
        routed_weight = jnp.where(in_first, weight_first, 0.0) + jnp.where(
            in_second, weight_second, 0.0
        )
        gated = jnp.dot(everyone, gate_weight[member], preferred_element_type=jnp.float32)
        upward = jnp.dot(everyone, up_weight[member], preferred_element_type=jnp.float32)
        activated = (jax.nn.silu(gated) * upward).astype(jnp.bfloat16)
        expert_out = jnp.dot(activated, down_weight[member], preferred_element_type=jnp.float32)
        summed = summed + routed_weight[:, None] * expert_out
    reduced = lax.psum_scatter(summed, "shard", scatter_dimension=0, tiled=True)
    expert_mix = lax.psum(reduced, "expert")
    return (stream + expert_mix).astype(jnp.bfloat16)


def solution(mesh):
    in_specs = (
        P("shard", None),
        P("shard", "expert", None),
        P("shard", None, "expert", None),
        P("shard", None, "expert", None),
        P("expert", "shard"),
        P(),
        P(),
        P(),
        P("expert", None, "shard"),
        P("expert", None, "shard"),
        P("expert", "shard", None),
    )
    out_specs = P("shard", None)
    return jax.shard_map(
        on_device, mesh=mesh, in_specs=in_specs, out_specs=out_specs, check_vma=False
    )
```

profile of v0, /device:TPU:0, one launch (start us, length us, event | category | flops | bytes accessed | tf_op | source)
XLA Modules:
  0.0 225.8 jit_solution(6295233523832174419)
XLA Ops:
  6.5 0.0 copy-start
  6.5 1.6 copy-done
  8.1 1.4 fusion.46
  9.5 0.2 fusion.79
  9.7 2.0 fusion.49
  11.8 15.7 %all_gather.6 = bf16[64,1024]{1,0:T(8,128)(2,1)S(1)} all-gather(bf16[8,1024]{1,0:T(8,128)(2,1)S(1)} %reshape.37), channel_id=1, replica_groups=mesh['expert'=4,'shard'=8] {'shard'}, dimensions={0}, use_global_device_ids=true | all-gather | bytes 147456 | tf_op jit(solution)/shard_map/all_gather | solution.py:34
  27.5 2.2 convolution_bitcast_fusion
  29.7 4.6 %all-to-all-start = ((f32[8,8,512]{2,1,0:T(8,128)}), f32[8,8,512]{2,1,0:T(8,128)S(1)}, u32[]{:S(2)}, u32[]{:S(2)}) async-start(f32[8,8,512]{2,1,0:T(8,128)} %convolution_bitcast_fusion), calls=%async_computation | async-start | bytes 262144 | tf_op jit(solution)/shard_map/all_to_all | solution.py:36
  34.3 0.0 all-reduce.3.cloned.1.call-start
  34.3 0.7 convert_element_type.27
  35.0 0.8 fusion.78
  35.8 5.2 %all-to-all-done = f32[8,8,512]{2,1,0:T(8,128)S(1)} async-done(((f32[8,8,512]{2,1,0:T(8,128)}), f32[8,8,512]{2,1,0:T(8,128)S(1)}, u32[]{:S(2)}, u32[]{:S(2)}) %all-to-all-start) | async-done | bytes 131104 | tf_op jit(solution)/shard_map/all_to_all | solution.py:36
  41.0 0.0 copy-start.4
  41.0 0.6 copy-done.4
  41.7 0.0 all-reduce.3.cloned.1.call-update
  41.7 0.0 reduce-scatter.2.cloned.1.call-start
  41.8 41.4 %all-reduce.3.cloned.1.call-done = f32[8,4096]{1,0:T(8,128)} async-done(((f32[8,4096]{1,0:T(8,128)}), f32[8,4096]{1,0:T(8,128)}) %all-reduce.3.cloned.1.call-update) | async-done | bytes 131088 | tf_op jit(solution)/shard_map/psum | solution.py:37
  83.2 1.1 multiply_reduce_fusion
  84.2 1.0 multiply_convert_fusion
  85.2 14.7 %all_gather.7 = bf16[64,4096]{1,0:T(8,128)(2,1)S(1)} all-gather(bf16[8,4096]{1,0:T(8,128)(2,1)S(1)} %multiply_convert_fusion), channel_id=1, replica_groups=mesh['expert'=4,'shard'=8] {'shard'}, dimensions={0}, use_global_device_ids=true | all-gather | bytes 589824 | tf_op jit(solution)/shard_map/all_gather | solution.py:41
  100.0 0.0 copy-start.5
  100.0 0.0 copy-start.6
  100.0 6.5 %fusion.5 = f32[64,1792]{1,0:T(8,128)S(1)} fusion(bf16[64,4096]{1,0:T(8,128)(2,1)S(1)} %all_gather.7, bf16[2,4096,1792]{2,1,0:T(8,128)(2,1)} %param.21), kind=kOutput, calls=%fused_computation.7 | convolution fusion | flops 939524096 | bytes 15663104 | tf_op jit(solution)/shard_map/dot_general | solution.py:58
  106.4 6.4 %fusion.11 = f32[64,1792]{1,0:T(8,128)S(1)} fusion(bf16[64,4096]{1,0:T(8,128)(2,1)S(1)} %all_gather.7, bf16[2,4096,1792]{2,1,0:T(8,128)(2,1)} %param.21), kind=kOutput, calls=%fused_computation.13 | convolution fusion | flops 939524096 | bytes 15663104 | tf_op jit(solution)/shard_map/dot_general | solution.py:58
  112.9 0.0 copy-done.5
  112.9 0.2 fusion.80
  113.2 0.7 gather_fusion
  113.9 0.7 gather_fusion.1
  114.6 0.0 copy-done.6
  114.7 13.1 %fusion.25 = f32[64,4096]{1,0:T(8,128)} fusion(bf16[2,1792,4096]{2,1,0:T(8,128)(2,1)} %param.23, bf16[64,4096]{1,0:T(8,128)(2,1)S(1)} %all_gather.7, bf16[2,4096,1792]{2,1,0:T(8,128)(2,1)} %param.22, f32[64]{0:T(128)S(1)} %fusion.73, f32[64,1792]{1,0:T(8,128)S(1)} %fusion.5), kind=kOutput, calls=%fused_computation.23 | convolution fusion | flops 1879998464 | bytes 31392000 | tf_op jit(solution)/shard_map/dot_general | solution.py:61
  127.8 0.0 copy-start.1
  127.8 0.0 copy-start.2
  127.8 0.0 copy-start.3
  127.8 13.6 %fusion.22 = f32[64,4096]{1,0:T(8,128)} fusion(f32[64,4096]{1,0:T(8,128)} %fusion.25, bf16[2,1792,4096]{2,1,0:T(8,128)(2,1)} %param.23, bf16[64,4096]{1,0:T(8,128)(2,1)S(1)} %all_gather.7, bf16[2,4096,1792]{2,1,0:T(8,128)(2,1)} %param.22, f32[64]{0:T(128)S(1)} %get-tuple-element.6, f32[64,1792]{1,0:T(8,128)S(1)} %fusion.11), kind=kOutput, calls=%fused_computation.22 | convolution fusion | flops 1880260608 | bytes 32440576 | tf_op jit(solution)/shard_map/dot_general | solution.py:61
  141.4 0.0 reduce-scatter.2.cloned.1.call-update
  141.5 0.0 all-reduce.5.cloned.1.call-start
  141.5 32.9 %reduce-scatter.2.cloned.1.call-done = f32[8,4096]{1,0:T(8,128)} async-done(((f32[64,4096]{1,0:T(8,128)}), f32[8,4096]{1,0:T(8,128)}) %reduce-scatter.2.cloned.1.call-update) | async-done | bytes 131088 | tf_op jit(solution)/shard_map/reduce_scatter | solution.py:63
  174.4 0.0 all-reduce.5.cloned.1.call-update
  174.4 43.3 %all-reduce.5.cloned.1.call-done = f32[8,4096]{1,0:T(8,128)} async-done(((f32[8,4096]{1,0:T(8,128)}), f32[8,4096]{1,0:T(8,128)}) %all-reduce.5.cloned.1.call-update) | async-done | bytes 131088 | tf_op jit(solution)/shard_map/psum | solution.py:64
  217.7 0.0 copy-done.2
  217.7 0.0 copy-done.3
  217.7 1.6 add_convert_fusion
  219.2 0.0 copy-done.1
  (8 shorter events, 0.1 us)
Async XLA Ops:
  6.5 1.6 copy-start
  29.7 11.3 %all-to-all-start = ((f32[8,8,512]{2,1,0:T(8,128)}), f32[8,8,512]{2,1,0:T(8,128)S(1)}, u32[]{:S(2)}, u32[]{:S(2)}) async-start(f32[8,8,512]{2,1,0:T(8,128)} %convolution_bitcast_fusion), calls=%async_computation | async-start | bytes 262144 | tf_op jit(solution)/shard_map/all_to_all | solution.py:36
  34.3 48.9 %all-reduce.3.cloned.1.call-start = ((), (), s32[]{:S(2)}) async-start(), calls=%async_computation.2 | async-start | bytes 262144 | tf_op jit(solution)/shard_map/psum | solution.py:37
  41.0 0.6 copy-start.4
  41.7 132.7 %reduce-scatter.2.cloned.1.call-start = ((), (), s32[]{:S(2)}) async-start(), calls=%async_computation.3 | async-start | bytes 1179648 | tf_op jit(solution)/shard_map/reduce_scatter | solution.py:63
  100.0 12.9 %copy-start.5 = (bf16[4096,8]{0,1:T(8,128)(2,1)S(1)}, bf16[4096,8]{0,1:T(8,128)(2,1)}, u32[]{:S(2)}) copy-start(bf16[4096,8]{0,1:T(8,128)(2,1)} %param.19) | copy-start | bytes 196612
  100.0 14.7 %copy-start.6 = (s32[64,2]{0,1:T(2,128)S(1)}, s32[64,2]{0,1:T(2,128)}, u32[]{:S(2)}) copy-start(s32[64,2]{0,1:T(2,128)} %param.20) | copy-start | bytes 1540
  127.8 91.4 %copy-start.1 = (bf16[8,512,2,128]{3,2,1,0:T(2,128)(2,1)S(1)}, bf16[8,512,2,128]{3,2,1,0:T(2,128)(2,1)}, u32[]{:S(2)}) copy-start(bf16[8,512,2,128]{3,2,1,0:T(2,128)(2,1)} %param.15) | copy-start | bytes 6291460
  127.8 89.9 %copy-start.2 = (f32[8,4096]{1,0:T(8,128)S(1)}, f32[8,4096]{1,0:T(8,128)}, u32[]{:S(2)}) copy-start(f32[8,4096]{1,0:T(8,128)} %all-reduce.3.cloned.1.call-done) | copy-start | bytes 393220
  127.8 89.9 %copy-start.3 = (bf16[8,4096]{1,0:T(8,128)(2,1)S(1)}, bf16[8,4096]{1,0:T(8,128)(2,1)}, u32[]{:S(2)}) copy-start(bf16[8,4096]{1,0:T(8,128)(2,1)} %param.13) | copy-start | bytes 196612
  141.5 76.2 %all-reduce.5.cloned.1.call-start = ((), (), s32[]{:S(2)}) async-start(), calls=%async_computation.4 | async-start | bytes 262144 | tf_op jit(solution)/shard_map/psum | solution.py:64
Sparse Core Ops, SparseCore 0:
  41.8 41.2 all-reduce.2
  141.6 32.7 reduce-scatter.1
  177.3 40.3 all-reduce.4
where the time goes:
time: 226 us
  waiting for transfers between devices  123 us (54%)
  matrix products  45.5 us (20%)
  blocking collectives  30.5 us (13%)
  between operations  13.2 us (6%)
  other arithmetic  5.35 us (2%)
  starting transfers between devices  4.72 us (2%)
  local copies, waits for them, and re-layouts  3.76 us (2%)
    psum x1, waiting for transfers between devices, on_device(): expert_mix = lax.psum(reduced, 'expert')  43.3 us
    psum x1, waiting for transfers between devices, on_device(): attn_out = lax.psum(partial_heads, 'expert')  41.4 us
    reduce_scatter x1, waiting for transfers between devices, on_device(): reduced = lax.psum_scatter(summed, 'shard', scatter_dimension=0, tiled=True)  32.9 us
    dot_general x2, matrix products, on_device(): jnp.dot(activated, down_weight[member], preferred_element_type=jnp.float32)  26.7 us
    all_gather x1, blocking collectives, on_device(): all_attended = lax.all_gather(attended, 'shard', axis=0, tiled=True)  15.7 us
    all_gather x1, blocking collectives, on_device(): everyone = lax.all_gather(normed, 'shard', axis=0, tiled=True)  14.7 us
    dot_general x2, matrix products, on_device(): jnp.dot(everyone, gate_weight[member], preferred_element_type=jnp.float32)  12.9 us
    all_to_all x1, waiting for transfers between devices, on_device(): lax.all_to_all(partial_cols, 'shard', split_axis=0, concat_axis=1, tiled=...  5.22 us
  transfers between devices with their start and end apart: 4, of which 4 were waited for; matrix products, arithmetic and copies ran while one was open for 1% of the time, Pallas kernels for 0%

commit v1 on v0

v1 whole, which is shorter than its diff:
```python
import functools
import math

import jax
import jax.numpy as jnp
from jax import lax
from jax.experimental import pallas as pl
from jax.experimental.pallas import tpu as pltpu
from jax.sharding import PartitionSpec as P

F32 = jnp.float32
BF16 = jnp.bfloat16
VMEM_BYTES = 61 * 1024 * 1024
DOWN = 256
LAG = 2


def layer_kernel(
    sizes,
    hidden_ref,
    queries_ref,
    key_ref,
    value_ref,
    out_weight_ref,
    gain_ref,
    router_ref,
    ids_ref,
    gate_ref,
    up_ref,
    down_ref,
    out_ref,
    ring,
    keys,
    values,
    proj,
    score,
    heads,
    att_all,
    hid_all,
    part_all,
    stream,
    owned,
    x_all,
    normed,
    route,
    act,
    part_out,
    part_in,
    group,
    ring_sem,
    kv_sem,
    proj_sem,
    att_s,
    att_r,
    hid_s,
    hid_r,
    part_s,
    part_r,
    x_s,
    x_r,
    own_s,
    own_r,
    a_s,
    a_r,
    b_s,
    b_r,
):
    shards, groups, depth, width, kv_local = sizes
    me = lax.axis_index("shard")
    ge = lax.axis_index("expert")
    count, features = hidden_ref.shape
    tokens = count * shards
    cols = features // shards
    members, _, hidden_units = gate_ref.shape
    per_member = hidden_units // width
    gu_pairs = members * per_member
    chunk = 2 * DOWN
    chunks = features // chunk
    total = gu_pairs + chunks
    heads_local, head_size = queries_ref.shape[1:]
    per_kv = heads_local // kv_local

    def shard_peer(d):
        return lax.rem(me + d, shards)

    def group_peer(d):
        return lax.rem(ge + d, groups)

    def to_shard(src, dst, ssem, rsem, peer):
        return pltpu.make_async_remote_copy(
            src_ref=src, dst_ref=dst, send_sem=ssem, recv_sem=rsem,
            device_id={"shard": peer}, device_id_type=pl.DeviceIdType.MESH,
        )

    def to_group(src, dst, ssem, rsem, peer):
        return pltpu.make_async_remote_copy(
            src_ref=src, dst_ref=dst, send_sem=ssem, recv_sem=rsem,
            device_id={"expert": peer}, device_id_type=pl.DeviceIdType.MESH,
        )

    def each(n, body):
        def step(i, carry):
            body(i)
            return carry

        lax.fori_loop(0, n, step, 0)

    def span(i, size):
        return pl.ds(pl.multiple_of(i * size, size), size)

    def gate_up_copies(pair):
        slot = lax.rem(pair, depth)
        member, j = lax.div(pair, per_member), lax.rem(pair, per_member)
        where = slice(None) if per_member == 1 else span(j, width)
        return [
            pltpu.make_async_copy(
                ref.at[member, :, where], ring.at[slot, k, 0:features, 0:width], ring_sem.at[slot, k]
            )
            for k, ref in enumerate((gate_ref, up_ref))
        ]

    def down_copies(pair):
        slot = lax.rem(pair, depth)
        c = pair - gu_pairs
        return [
            pltpu.make_async_copy(
                down_ref.at[m, :, span(2 * c + k, DOWN)],
                ring.at[slot, k, m * hidden_units:(m + 1) * hidden_units, 0:DOWN],
                ring_sem.at[slot, k * members + m],
            )
            for k in range(2)
            for m in range(members)
        ]

    def start_pair(pair):
        @pl.when(pair < gu_pairs)
        def _():
            for copy in gate_up_copies(pair):
                copy.start()

        @pl.when(jnp.logical_and(pair >= gu_pairs, pair < total))
        def _():
            for copy in down_copies(pair):
                copy.start()

    barrier = pltpu.get_barrier_semaphore()
    each(shards - 1, lambda d: pl.semaphore_signal(
        barrier, 1, device_id={"shard": shard_peer(d + 1)}, device_id_type=pl.DeviceIdType.MESH))
    each(groups - 1, lambda d: pl.semaphore_signal(
        barrier, 1, device_id={"expert": group_peer(d + 1)}, device_id_type=pl.DeviceIdType.MESH))

    def key_copy(t):
        return pltpu.make_async_copy(key_ref.at[t], keys.at[t], kv_sem.at[0, t])

    def value_copy(t):
        return pltpu.make_async_copy(value_ref.at[t], values.at[t], kv_sem.at[1, t])

    each(count, lambda t: key_copy(t).start())
    each(count, lambda t: value_copy(t).start())
    proj_copy = pltpu.make_async_copy(out_weight_ref, proj, proj_sem)
    proj_copy.start()
    each(depth, start_pair)

    for t in range(count):
        key_copy(t).wait()
        score[t * heads_local:(t + 1) * heads_local, :] = lax.dot_general(
            queries_ref[t], keys[t], (((1,), (1,)), ((), ())), preferred_element_type=F32
        )
    s = score[...] * (1.0 / math.sqrt(head_size))
    row = lax.broadcasted_iota(jnp.int32, s.shape, 0)
    col = lax.broadcasted_iota(jnp.int32, s.shape, 1)
    mine = lax.rem(col, kv_local) == lax.div(lax.rem(row, heads_local), per_kv)
    s = jnp.where(mine, s, -1e30)
    e = jnp.exp(s - jnp.max(s, axis=1, keepdims=True))
    score[...] = e / jnp.sum(e, axis=1, keepdims=True)
    for t in range(count):
        value_copy(t).wait()
        attended = jnp.dot(
            score[t * heads_local:(t + 1) * heads_local, :].astype(BF16), values[t],
            preferred_element_type=F32,
        )
        for h in range(heads_local):
            heads[t:t + 1, h * head_size:(h + 1) * head_size] = attended[h:h + 1, :]
    att_all[me] = heads[...].astype(BF16)

    pl.semaphore_wait(barrier, shards - 1 + groups - 1)

    def att_copy(slot, peer, k):
        return to_shard(att_all.at[slot], att_all.at[slot], att_s.at[k], att_r.at[slot], peer)

    def hid_copy(peer, slot, k):
        return to_shard(
            hidden_ref.at[:, span(peer, cols)], hid_all.at[slot], hid_s.at[k], hid_r.at[slot], peer
        )

    def send_first(d):
        att_copy(me, shard_peer(d + 1), d).start()

    def send_hidden(d):
        hid_copy(shard_peer(d + 1), me, d).start()

    each(shards - 1, send_first)
    each(shards - 1, send_hidden)
    hid_all[me] = hidden_ref[:, span(me, cols)]
    proj_copy.wait()
    each(shards - 1, lambda d: att_copy(shard_peer(d + 1), me, d).wait_recv())

    gathered = att_all[...].astype(F32).reshape(tokens, heads_local * head_size).astype(BF16)
    part_all[ge] = jnp.dot(gathered, proj[...], preferred_element_type=F32).astype(BF16)

    def part_copy(slot, peer, k):
        return to_group(part_all.at[slot], part_all.at[slot], part_s.at[k], part_r.at[slot], peer)

    each(groups - 1, lambda d: part_copy(ge, group_peer(d + 1), d).start())
    each(shards - 1, lambda d: hid_copy(me, shard_peer(d + 1), d).wait_recv())
    each(groups - 1, lambda d: part_copy(group_peer(d + 1), ge, d).wait_recv())
    summed = hid_all[...].astype(F32).reshape(tokens, cols)
    for g in range(groups):
        summed = summed + part_all[g].astype(F32)
    stream[...] = summed
    x_all[:, span(me, cols)] = summed.astype(BF16)

    def x_copy(block, peer, k):
        return to_shard(
            x_all.at[:, span(block, cols)], x_all.at[:, span(block, cols)],
            x_s.at[k], x_r.at[block], peer,
        )

    def own_copy(peer, block, k):
        return to_shard(
            stream.at[span(peer, count), :], owned.at[:, span(block, cols)],
            own_s.at[k], own_r.at[block], peer,
        )

    each(shards - 1, lambda d: x_copy(me, shard_peer(d + 1), d).start())
    each(shards - 1, lambda d: own_copy(shard_peer(d + 1), me, d).start())
    owned[:, span(me, cols)] = stream[span(me, count), :]
    each(shards - 1, lambda d: x_copy(shard_peer(d + 1), me, d).wait_recv())

    square = jnp.zeros((tokens, 1), F32)
    for c in range(chunks):
        x = x_all[:, c * chunk:(c + 1) * chunk].astype(F32)
        square = square + jnp.sum(x * x, axis=1, keepdims=True)
    scale = lax.rsqrt(square / features + 1e-05)
    gain = gain_ref[...].astype(F32)
    lanes = gain.shape[1]
    for c in range(gain.shape[0]):
        part = slice(c * lanes, (c + 1) * lanes)
        normed[:, part] = (x_all[:, part].astype(F32) * scale * gain[c:c + 1]).astype(BF16)

    logits = lax.dot_general(
        normed[...], router_ref[...], (((1,), (1,)), ((), ())), preferred_element_type=F32
    )
    diagonal = lax.broadcasted_iota(jnp.int32, (tokens, tokens), 0) == lax.broadcasted_iota(
        jnp.int32, (tokens, tokens), 1
    )
    first, second = (
        jnp.sum(
            jnp.where(diagonal, ids_ref[k:k + 1, :].astype(F32), 0.0), axis=1, keepdims=True
        ).astype(jnp.int32)
        for k in range(2)
    )
    lane = lax.broadcasted_iota(jnp.int32, logits.shape, 1)
    top_first = jnp.sum(jnp.where(lane == first, logits, 0.0), axis=1, keepdims=True)
    top_second = jnp.sum(jnp.where(lane == second, logits, 0.0), axis=1, keepdims=True)
    weight_first = 1.0 / (1.0 + jnp.exp(top_second - top_first))
    weight_second = 1.0 / (1.0 + jnp.exp(top_first - top_second))
    for m in range(members):
        expert = ge * members + m
        route[m] = jnp.broadcast_to(
            jnp.where(first == expert, weight_first, 0.0)
            + jnp.where(second == expert, weight_second, 0.0),
            (tokens, 128),
        )

    def gate_up(pair):
        slot = lax.rem(pair, depth)
        member, j = lax.div(pair, per_member), lax.rem(pair, per_member)
        for copy in gate_up_copies(pair):
            copy.wait()
        gated = jnp.dot(
            normed[...], ring[slot, 0, 0:features, 0:width], preferred_element_type=F32
        )
        upward = jnp.dot(
            normed[...], ring[slot, 1, 0:features, 0:width], preferred_element_type=F32
        )
        value = gated * (1.0 / (1.0 + jnp.exp(-gated))) * upward * route[member][:, 0:1]
        where = slice(None) if per_member == 1 else span(j, width)
        act[member, :, where] = value.astype(BF16)
        start_pair(pair + depth)

    each(gu_pairs, gate_up)

    def a_copy(c, source, dest, peer, k):
        return to_shard(
            part_out.at[dest, :, span(c, chunk)], part_in.at[source, :, span(c, chunk)],
            a_s.at[k, c], a_r.at[source, c], peer,
        )

    def b_copy(c, slot, peer, k):
        ref = group.at[slot, :, span(c, chunk)]
        return to_group(ref, ref, b_s.at[k, c], b_r.at[slot, c], peer)

    def finish_shards(c):
        each(shards - 1, lambda d: a_copy(c, shard_peer(d + 1), me, me, d).wait_recv())
        mix = part_out[me, :, span(c, chunk)].astype(F32)
        mix = lax.fori_loop(
            1, shards,
            lambda d, got: got + part_in[shard_peer(d), :, span(c, chunk)].astype(F32), mix,
        )
        group[ge, :, span(c, chunk)] = mix.astype(BF16)
        each(groups - 1, lambda d: b_copy(c, ge, group_peer(d + 1), d).start())

    def down(c):
        pair = gu_pairs + c
        slot = lax.rem(pair, depth)
        for copy in down_copies(pair):
            copy.wait()
        for k in range(2):
            y = jnp.zeros((tokens, DOWN), F32)
            for m in range(members):
                y = y + jnp.dot(
                    act[m],
                    ring[slot, k, m * hidden_units:(m + 1) * hidden_units, 0:DOWN],
                    preferred_element_type=F32,
                )
            part_out[:, :, span(2 * c + k, DOWN)] = y.reshape(shards, count, DOWN).astype(BF16)
        each(shards - 1, lambda d: a_copy(c, me, shard_peer(d + 1), shard_peer(d + 1), d).start())
        start_pair(pair + depth)

        @pl.when(c >= LAG)
        def _():
            finish_shards(c - LAG)

    each(chunks, down)
    each(LAG, lambda i: finish_shards(chunks - LAG + i))
    each(shards - 1, lambda d: own_copy(me, shard_peer(d + 1), d).wait_recv())

    def finish(c):
        each(groups - 1, lambda d: b_copy(c, group_peer(d + 1), ge, d).wait_recv())
        result = group[0, :, span(c, chunk)].astype(F32)
        for g in range(1, groups):
            result = result + group[g, :, span(c, chunk)].astype(F32)
        out_ref[:, span(c, chunk)] = (owned[:, span(c, chunk)] + result).astype(BF16)

    each(chunks, finish)

    def sent(d):
        att_copy(me, shard_peer(d + 1), d).wait_send()
        hid_copy(shard_peer(d + 1), me, d).wait_send()
        x_copy(me, shard_peer(d + 1), d).wait_send()
        own_copy(shard_peer(d + 1), me, d).wait_send()
        each(chunks, lambda c: a_copy(c, me, shard_peer(d + 1), shard_peer(d + 1), d).wait_send())

    def sent_group(d):
        part_copy(ge, group_peer(d + 1), d).wait_send()
        each(chunks, lambda c: b_copy(c, ge, group_peer(d + 1), d).wait_send())

    each(shards - 1, sent)
    each(groups - 1, sent_group)


def on_device(
    shards,
    groups,
    hidden,
    queries,
    key_cache,
    value_cache,
    out_weight,
    norm_gain,
    router,
    expert_ids,
    gate_weight,
    up_weight,
    down_weight,
):
    count, features = hidden.shape
    _, heads_local, head_size = queries.shape
    _, positions, kv_local, _ = key_cache.shape
    members, _, hidden_units = gate_weight.shape
    tokens = count * shards
    cols = features // shards
    rows = positions * kv_local
    width = 256 if hidden_units % 256 == 0 else hidden_units
    lanes = max(width, DOWN)
    deep = max(features, members * hidden_units)
    chunks = features // (2 * DOWN)
    total = members * (hidden_units // width) + chunks
    pair_bytes = 2 * 2 * deep * (-(-lanes // 128) * 128)
    fixed = 2 * (
        2 * count * rows * head_size + out_weight.size + 4 * tokens * features
        + (groups + 2) * tokens * cols + members * tokens * hidden_units
        + (2 * count + groups * count) * features + 2 * count * heads_local * rows
    )
    depth = min(total, (VMEM_BYTES - fixed) // pair_bytes)
    sizes = (shards, groups, depth, width, kv_local)
    vmem = pl.BlockSpec(memory_space=pltpu.VMEM)
    hbm = pl.BlockSpec(memory_space=pl.ANY)
    sem = pltpu.SemaphoreType.DMA
    return pl.pallas_call(
        functools.partial(layer_kernel, sizes),
        out_shape=jax.ShapeDtypeStruct((count, features), BF16),
        in_specs=[vmem, vmem, hbm, hbm, hbm, vmem, vmem, vmem, hbm, hbm, hbm],
        out_specs=vmem,
        scratch_shapes=[
            pltpu.VMEM((depth, 2, deep, lanes), BF16),
            pltpu.VMEM((count, rows, head_size), BF16),
            pltpu.VMEM((count, rows, head_size), BF16),
            pltpu.VMEM(out_weight.shape, BF16),
            pltpu.VMEM((count * heads_local, rows), F32),
            pltpu.VMEM((count, heads_local * head_size), F32),
            pltpu.VMEM((shards, count, heads_local * head_size), BF16),
            pltpu.VMEM((shards, count, cols), BF16),
            pltpu.VMEM((groups, tokens, cols), BF16),
            pltpu.VMEM((tokens, cols), F32),
            pltpu.VMEM((count, features), F32),
            pltpu.VMEM((tokens, features), BF16),
            pltpu.VMEM((tokens, features), BF16),
            pltpu.VMEM((members, tokens, 128), F32),
            pltpu.VMEM((members, tokens, hidden_units), BF16),
            pltpu.VMEM((shards, count, features), BF16),
            pltpu.VMEM((shards, count, features), BF16),
            pltpu.VMEM((groups, count, features), BF16),
            sem((depth, 2 * members)),
            sem((2, count)),
            sem,
            sem((shards,)),
            sem((shards,)),
            sem((shards,)),
            sem((shards,)),
            sem((groups,)),
            sem((groups,)),
            sem((shards,)),
            sem((shards,)),
            sem((shards,)),
            sem((shards,)),
            sem((shards, chunks)),
            sem((shards, chunks)),
            sem((groups, chunks)),
            sem((groups, chunks)),
        ],
        compiler_params=pltpu.CompilerParams(
            collective_id=0, has_side_effects=True, vmem_limit_bytes=67043328
        ),
        name="layer",
    )(
        hidden,
        queries,
        key_cache.reshape(count, rows, head_size),
        value_cache.reshape(count, rows, head_size),
        out_weight,
        norm_gain.reshape(features // 128, 128),
        router.T,
        expert_ids.T,
        gate_weight,
        up_weight,
        down_weight,
    )


def solution(mesh):
    in_specs = (
        P("shard", None),
        P("shard", "expert", None),
        P("shard", None, "expert", None),
        P("shard", None, "expert", None),
        P("expert", "shard"),
        P(),
        P(),
        P(),
        P("expert", None, "shard"),
        P("expert", None, "shard"),
        P("expert", "shard", None),
    )
    body = functools.partial(on_device, mesh.shape["shard"], mesh.shape["expert"])
    return jax.shard_map(
        body, mesh=mesh, in_specs=in_specs, out_specs=P("shard", None), check_vma=False
    )
```

time: 226 us -> 70.3 us (0.31)
  waiting for transfers between devices: 123 us -> 0 us
  Pallas kernels: 0 us -> 68.6 us
  matrix products: 45.5 us -> 0 us
  blocking collectives: 30.5 us -> 0 us
  between operations: 13.2 us -> 0.01 us
  other arithmetic: 5.35 us -> 0 us
  starting transfers between devices: 4.72 us -> 0 us
  local copies, waits for them, and re-layouts: 3.76 us -> 1.47 us
    psum x2 -> x0, waiting for transfers between devices: 84.7 us -> none  [the longest x1 43.3 us: on_device(): expert_mix = lax.psum(reduced, 'expert')]
    pallas_call x0 -> x1, Pallas kernels: none -> 68.6 us  [on_device(): pl.pallas_call(functools.partial(layer_kernel, sizes), out_shape=jax.Shap...]
    dot_general x8 -> x0, matrix products: 45.5 us -> none  [the longest x2 26.7 us: on_device(): jnp.dot(activated, down_weight[member], preferred_element_type=jnp.float32)]
    reduce_scatter x1 -> x0, waiting for transfers between devices: 32.9 us -> none  [on_device(): reduced = lax.psum_scatter(summed, 'shard', scatter_dimension=0, tiled=True)]
    all_gather x2 -> x0, blocking collectives: 30.5 us -> none  [the longest x1 15.7 us: on_device(): all_attended = lax.all_gather(attended, 'shard', axis=0, tiled=True)]
    all_to_all x1 -> x0, waiting for transfers between devices: 5.22 us -> none  [on_device(): lax.all_to_all(partial_cols, 'shard', split_axis=0, concat_axis=1, tiled=...]
    all_to_all x1 -> x0, starting transfers between devices: 4.6 us -> none  [on_device(): lax.all_to_all(partial_cols, 'shard', split_axis=0, concat_axis=1, tiled=...]
    convert_element_type x3 -> x0, other arithmetic: 3.25 us -> none  [the longest x2 1.7 us: on_device(): normed = (scaled * norm_gain.astype(jnp.float32)).astype(jnp.bfloat16)]
  transfers between devices with their start and end apart: 4 -> 0, of which waited for: 4 -> 0; matrix products, arithmetic and copies ran while one was open for 1% -> 0% of each run, Pallas kernels for 0% -> 0%
where the time goes in v1:
time: 70.3 us; the launch traced here: 70.1 us
  Pallas kernels  68.6 us (98%)
  local copies, waits for them, and re-layouts  1.47 us (2%)
    pallas_call x1, Pallas kernels, on_device(): pl.pallas_call(functools.partial(layer_kernel, sizes), out_shape=jax.Shap...  68.6 us
    unnamed x1, local copies, waits for them, and re-layouts  1.47 us

profile of v1, /device:TPU:0, one launch (start us, length us, event | category | flops | bytes accessed | tf_op | source)
XLA Modules:
  0.0 70.1 jit_solution(8169694321405488750)
XLA Ops:
  0.0 68.6 %layer.1 = bf16[8,4096]{1,0:T(8,128)(2,1)} custom-call(bf16[8,4096]{1,0:T(8,128)(2,1)} %hidden_ref.1, bf16[8,8,128]{2,1,0:T(8,128)(2,1)} %queries_ref.1, bf16[8,1024,128]{2,1,0:T(8,128)(2,1)} %bitcast.5, bf16[8,1024,128]{2,1,0:T(8,128)(2,1)} %bitcast.6, bf16[1024,512]{1,0:T(8,128)(2,1)} %out_weight_ref.1, bf16[32,128]{1,0:T(8,128)(2,1)} %bitcast.8, ...), custom_call_target="tpu_custom_call" | custom-call | tf_op jit(solution)/shard_map/layer/pallas_call | solution.py:401
  68.6 1.5 %copy.13 = bf16[8,4096]{1,0:T(8,128)(2,1)} copy(bf16[8,4096]{1,0:T(8,128)(2,1)} %layer.1) | data formatting | bytes 131072

commit v2 on v1

--- a/solution.py
+++ b/solution.py
@@ -12,7 +12,6 @@
 BF16 = jnp.bfloat16
 VMEM_BYTES = 61 * 1024 * 1024
 DOWN = 256
-LAG = 2
 
 
 def layer_kernel(
@@ -37,16 +36,18 @@
     heads,
     att_all,
     hid_all,
-    part_all,
-    stream,
-    owned,
+    part_send,
+    part_recv,
     x_all,
     normed,
     route,
     act,
     part_out,
-    part_in,
+    core_in,
+    core_sum,
+    chip_in,
     group,
+    final,
     ring_sem,
     kv_sem,
     proj_sem,
@@ -56,14 +57,18 @@
     hid_r,
     part_s,
     part_r,
-    x_s,
+    x_z,
+    x_g,
+    x_c,
     x_r,
-    own_s,
-    own_r,
+    i_s,
+    i_r,
     a_s,
     a_r,
     b_s,
     b_r,
+    f_s,
+    f_r,
 ):
     shards, groups, depth, width, kv_local = sizes
     me = lax.axis_index("shard")
@@ -79,12 +84,20 @@
     total = gu_pairs + chunks
     heads_local, head_size = queries_ref.shape[1:]
     per_kv = heads_local // kv_local
+    quarter = shards // groups
+    pairs = shards // 2
+    core = lax.rem(me, 2)
+    chip = lax.div(me, 2)
+    sibling = me + 1 - 2 * core
 
     def shard_peer(d):
         return lax.rem(me + d, shards)
 
     def group_peer(d):
         return lax.rem(ge + d, groups)
+
+    def chip_peer(d):
+        return lax.rem(chip + d, pairs)
 
     def to_shard(src, dst, ssem, rsem, peer):
         return pltpu.make_async_remote_copy(
@@ -161,6 +174,21 @@
     proj_copy.start()
     each(depth, start_pair)
 
+    pl.semaphore_wait(barrier, shards - 1 + groups - 1)
+
+    def hid_copy(peer, slot, k):
+        return to_shard(
+            hidden_ref.at[:, span(peer, cols)], hid_all.at[slot], hid_s.at[k], hid_r.at[slot], peer
+        )
+
+    slot_mine = lax.rem(me, quarter)
+    sends_hidden = lax.div(me, quarter) == ge
+
+    @pl.when(sends_hidden)
+    def _():
+        each(shards - 1, lambda d: hid_copy(shard_peer(d + 1), slot_mine, d).start())
+        hid_all[slot_mine] = hidden_ref[:, span(me, cols)]
+
     for t in range(count):
         key_copy(t).wait()
         score[t * heads_local:(t + 1) * heads_local, :] = lax.dot_general(
@@ -183,70 +211,92 @@
             heads[t:t + 1, h * head_size:(h + 1) * head_size] = attended[h:h + 1, :]
     att_all[me] = heads[...].astype(BF16)
 
-    pl.semaphore_wait(barrier, shards - 1 + groups - 1)
-
     def att_copy(slot, peer, k):
         return to_shard(att_all.at[slot], att_all.at[slot], att_s.at[k], att_r.at[slot], peer)
 
-    def hid_copy(peer, slot, k):
-        return to_shard(
-            hidden_ref.at[:, span(peer, cols)], hid_all.at[slot], hid_s.at[k], hid_r.at[slot], peer
-        )
-
     def send_first(d):
         att_copy(me, shard_peer(d + 1), d).start()
 
-    def send_hidden(d):
-        hid_copy(shard_peer(d + 1), me, d).start()
-
     each(shards - 1, send_first)
-    each(shards - 1, send_hidden)
-    hid_all[me] = hidden_ref[:, span(me, cols)]
     proj_copy.wait()
     each(shards - 1, lambda d: att_copy(shard_peer(d + 1), me, d).wait_recv())
 
     gathered = att_all[...].astype(F32).reshape(tokens, heads_local * head_size).astype(BF16)
-    part_all[ge] = jnp.dot(gathered, proj[...], preferred_element_type=F32).astype(BF16)
+    partial = jnp.dot(gathered, proj[...], preferred_element_type=F32)
+    part_send[...] = partial.reshape(shards, count, cols).astype(BF16)
 
     def part_copy(slot, peer, k):
-        return to_group(part_all.at[slot], part_all.at[slot], part_s.at[k], part_r.at[slot], peer)
+        return to_group(
+            part_send.at[pl.ds(peer * quarter, quarter)], part_recv.at[slot],
+            part_s.at[k], part_r.at[slot], peer,
+        )
 
     each(groups - 1, lambda d: part_copy(ge, group_peer(d + 1), d).start())
-    each(shards - 1, lambda d: hid_copy(me, shard_peer(d + 1), d).wait_recv())
-    each(groups - 1, lambda d: part_copy(group_peer(d + 1), ge, d).wait_recv())
-    summed = hid_all[...].astype(F32).reshape(tokens, cols)
-    for g in range(groups):
-        summed = summed + part_all[g].astype(F32)
-    stream[...] = summed
-    x_all[:, span(me, cols)] = summed.astype(BF16)
-
-    def x_copy(block, peer, k):
-        return to_shard(
-            x_all.at[:, span(block, cols)], x_all.at[:, span(block, cols)],
-            x_s.at[k], x_r.at[block], peer,
-        )
-
-    def own_copy(peer, block, k):
-        return to_shard(
-            stream.at[span(peer, count), :], owned.at[:, span(block, cols)],
-            own_s.at[k], own_r.at[block], peer,
-        )
-
-    each(shards - 1, lambda d: x_copy(me, shard_peer(d + 1), d).start())
-    each(shards - 1, lambda d: own_copy(shard_peer(d + 1), me, d).start())
-    owned[:, span(me, cols)] = stream[span(me, count), :]
-    each(shards - 1, lambda d: x_copy(shard_peer(d + 1), me, d).wait_recv())
+
+    def hidden_in(i):
+        @pl.when(ge * quarter + i != me)
+        def _():
+            hid_copy(sibling, i, 0).wait_recv()
+
+    each(quarter, hidden_in)
+    summed = hid_all[...].astype(F32) + part_send[pl.ds(ge * quarter, quarter)].astype(F32)
+    each(groups - 1, lambda d: part_copy(group_peer(d + 1), group_peer(d + 1), d).wait_recv())
+    for d in range(1, groups):
+        summed = summed + part_recv[group_peer(d)].astype(F32)
+    x_all[pl.ds(ge * quarter, quarter), :, span(me, cols)] = summed.astype(BF16)
+
+    def x_block(g, s):
+        return x_all.at[pl.ds(g * quarter, quarter), :, span(s, cols)]
+
+    def x_chip(s, peer, k):
+        return to_shard(x_block(ge, s), x_block(ge, s), x_z.at[k], x_r.at[ge, s], peer)
+
+    def x_group(g, s, d, j):
+        return to_group(
+            x_block(g, s), x_block(g, s), x_g.at[d, j], x_r.at[g, s], group_peer(d + 1)
+        )
+
+    def x_core(g, s, d, j):
+        return to_shard(x_block(g, s), x_block(g, s), x_c.at[d, j], x_r.at[g, s], sibling)
+
+    def like(j):
+        return 2 * chip_peer(j) + core
+
+    def pass_on(j):
+        each(groups - 1, lambda d: x_group(ge, like(j), d, j).start())
+        x_core(ge, like(j), 0, j).start()
+
+    each(pairs - 1, lambda d: x_chip(me, like(d + 1), d).start())
+    pass_on(0)
+
+    def arrived(d):
+        x_chip(like(d + 1), sibling, d).wait_recv()
+        pass_on(d + 1)
+
+    each(pairs - 1, arrived)
+
+    def across(j):
+        def one(d):
+            x_group(group_peer(d + 1), like(j), d, j).wait_recv()
+            x_core(group_peer(d + 1), like(j), d + 1, j).start()
+
+        each(groups - 1, one)
+
+    each(pairs, across)
+    each(pairs, lambda j: each(groups, lambda d: x_core(
+        group_peer(d), like(j) + 1 - 2 * core, d, j).wait_recv()))
 
     square = jnp.zeros((tokens, 1), F32)
     for c in range(chunks):
-        x = x_all[:, c * chunk:(c + 1) * chunk].astype(F32)
+        x = x_all[:, :, c * chunk:(c + 1) * chunk].astype(F32).reshape(tokens, chunk)
         square = square + jnp.sum(x * x, axis=1, keepdims=True)
     scale = lax.rsqrt(square / features + 1e-05)
     gain = gain_ref[...].astype(F32)
     lanes = gain.shape[1]
     for c in range(gain.shape[0]):
         part = slice(c * lanes, (c + 1) * lanes)
-        normed[:, part] = (x_all[:, part].astype(F32) * scale * gain[c:c + 1]).astype(BF16)
+        x = x_all[:, :, part].astype(F32).reshape(tokens, lanes)
+        normed[:, part] = (x * scale * gain[c:c + 1]).astype(BF16)
 
     logits = lax.dot_general(
         normed[...], router_ref[...], (((1,), (1,)), ((), ())), preferred_element_type=F32
@@ -291,25 +341,53 @@
 
     each(gu_pairs, gate_up)
 
-    def a_copy(c, source, dest, peer, k):
+    half = DOWN
+
+    def core_copy(c):
         return to_shard(
-            part_out.at[dest, :, span(c, chunk)], part_in.at[source, :, span(c, chunk)],
-            a_s.at[k, c], a_r.at[source, c], peer,
+            part_out.at[:, :, span(2 * c + 1 - core, half)], core_in.at[:, :, span(c, half)],
+            i_s.at[c], i_r.at[c], sibling,
+        )
+
+    def chip_copy(c, slot, dest, k):
+        return to_shard(
+            core_sum.at[pl.ds(2 * dest, 2), :, span(c, half)], chip_in.at[slot, :, :, span(c, half)],
+            a_s.at[k, c], a_r.at[slot, c], 2 * dest + core,
         )
 
     def b_copy(c, slot, peer, k):
-        ref = group.at[slot, :, span(c, chunk)]
+        ref = group.at[slot, :, :, span(c, half)]
         return to_group(ref, ref, b_s.at[k, c], b_r.at[slot, c], peer)
 
-    def finish_shards(c):
-        each(shards - 1, lambda d: a_copy(c, shard_peer(d + 1), me, me, d).wait_recv())
-        mix = part_out[me, :, span(c, chunk)].astype(F32)
-        mix = lax.fori_loop(
-            1, shards,
-            lambda d, got: got + part_in[shard_peer(d), :, span(c, chunk)].astype(F32), mix,
-        )
-        group[ge, :, span(c, chunk)] = mix.astype(BF16)
+    def final_copy(c, block):
+        ref = final.at[block, :, span(2 * c + 1 - block, half)]
+        return to_shard(ref, ref, f_s.at[c], f_r.at[c], sibling)
+
+    def sum_cores(c):
+        core_copy(c).wait_recv()
+        core_sum[:, :, span(c, half)] = (
+            part_out[:, :, span(2 * c + core, half)].astype(F32)
+            + core_in[:, :, span(c, half)].astype(F32)
+        ).astype(BF16)
+        each(pairs - 1, lambda d: chip_copy(c, chip, chip_peer(d + 1), d).start())
+
+    def sum_chips(c):
+        each(pairs - 1, lambda d: chip_copy(c, chip_peer(d + 1), chip_peer(d + 1), d).wait_recv())
+        mix = core_sum[pl.ds(2 * chip, 2), :, span(c, half)].astype(F32)
+        for d in range(1, pairs):
+            mix = mix + chip_in[chip_peer(d), :, :, span(c, half)].astype(F32)
+        group[ge, :, :, span(c, half)] = mix.astype(BF16)
         each(groups - 1, lambda d: b_copy(c, ge, group_peer(d + 1), d).start())
+
+    def sum_groups(c):
+        each(groups - 1, lambda d: b_copy(c, group_peer(d + 1), group_peer(d + 1), d).wait_recv())
+        mix = group[0, :, :, span(c, half)].astype(F32)
+        for g in range(1, groups):
+            mix = mix + group[g, :, :, span(c, half)].astype(F32)
+        where = span(2 * c + core, half)
+        mix = mix + x_all[pl.ds(2 * chip, 2), :, where].astype(F32)
+        final[:, :, where] = mix.astype(BF16)
+        final_copy(c, 1 - core).start()
 
     def down(c):
         pair = gu_pairs + c
@@ -325,39 +403,42 @@
                     preferred_element_type=F32,
                 )
             part_out[:, :, span(2 * c + k, DOWN)] = y.reshape(shards, count, DOWN).astype(BF16)
-        each(shards - 1, lambda d: a_copy(c, me, shard_peer(d + 1), shard_peer(d + 1), d).start())
+        core_copy(c).start()
         start_pair(pair + depth)
 
-        @pl.when(c >= LAG)
+    def stage(t):
+        @pl.when(t < chunks)
         def _():
-            finish_shards(c - LAG)
-
-    each(chunks, down)
-    each(LAG, lambda i: finish_shards(chunks - LAG + i))
-    each(shards - 1, lambda d: own_copy(me, shard_peer(d + 1), d).wait_recv())
-
-    def finish(c):
-        each(groups - 1, lambda d: b_copy(c, group_peer(d + 1), ge, d).wait_recv())
-        result = group[0, :, span(c, chunk)].astype(F32)
-        for g in range(1, groups):
-            result = result + group[g, :, span(c, chunk)].astype(F32)
-        out_ref[:, span(c, chunk)] = (owned[:, span(c, chunk)] + result).astype(BF16)
-
-    each(chunks, finish)
-
-    def sent(d):
-        att_copy(me, shard_peer(d + 1), d).wait_send()
-        hid_copy(shard_peer(d + 1), me, d).wait_send()
-        x_copy(me, shard_peer(d + 1), d).wait_send()
-        own_copy(shard_peer(d + 1), me, d).wait_send()
-        each(chunks, lambda c: a_copy(c, me, shard_peer(d + 1), shard_peer(d + 1), d).wait_send())
-
-    def sent_group(d):
-        part_copy(ge, group_peer(d + 1), d).wait_send()
-        each(chunks, lambda c: b_copy(c, ge, group_peer(d + 1), d).wait_send())
-
-    each(shards - 1, sent)
-    each(groups - 1, sent_group)
+            down(t)
+
+        for lag, work in ((1, sum_cores), (2, sum_chips), (3, sum_groups)):
+            @pl.when(jnp.logical_and(t >= lag, t < chunks + lag))
+            def _():
+                work(t - lag)
+
+    each(chunks + 3, stage)
+    each(chunks, lambda c: final_copy(c, core).wait_recv())
+    out_ref[...] = final[core]
+
+    each(shards - 1, lambda d: att_copy(me, shard_peer(d + 1), d).wait_send())
+
+    @pl.when(sends_hidden)
+    def _():
+        each(shards - 1, lambda d: hid_copy(shard_peer(d + 1), slot_mine, d).wait_send())
+
+    each(groups - 1, lambda d: part_copy(ge, group_peer(d + 1), d).wait_send())
+    each(pairs - 1, lambda d: x_chip(me, like(d + 1), d).wait_send())
+    each(pairs, lambda j: each(groups - 1, lambda d: x_group(ge, like(j), d, j).wait_send()))
+    each(pairs, lambda j: each(groups, lambda d: x_core(
+        group_peer(d), like(j), d, j).wait_send()))
+
+    def sent(c):
+        core_copy(c).wait_send()
+        final_copy(c, 1 - core).wait_send()
+        each(pairs - 1, lambda d: chip_copy(c, chip, chip_peer(d + 1), d).wait_send())
+        each(groups - 1, lambda d: b_copy(c, ge, group_peer(d + 1), d).wait_send())
+
+    each(chunks, sent)
 
 
 def on_device(
@@ -411,34 +492,40 @@
             pltpu.VMEM((count * heads_local, rows), F32),
             pltpu.VMEM((count, heads_local * head_size), F32),
             pltpu.VMEM((shards, count, heads_local * head_size), BF16),
+            pltpu.VMEM((shards // groups, count, cols), BF16),
             pltpu.VMEM((shards, count, cols), BF16),
-            pltpu.VMEM((groups, tokens, cols), BF16),
-            pltpu.VMEM((tokens, cols), F32),
-            pltpu.VMEM((count, features), F32),
-            pltpu.VMEM((tokens, features), BF16),
+            pltpu.VMEM((groups, shards // groups, count, cols), BF16),
+            pltpu.VMEM((shards, count, features), BF16),
             pltpu.VMEM((tokens, features), BF16),
             pltpu.VMEM((members, tokens, 128), F32),
             pltpu.VMEM((members, tokens, hidden_units), BF16),
             pltpu.VMEM((shards, count, features), BF16),
-            pltpu.VMEM((shards, count, features), BF16),
-            pltpu.VMEM((groups, count, features), BF16),
+            pltpu.VMEM((shards, count, features // 2), BF16),
+            pltpu.VMEM((shards, count, features // 2), BF16),
+            pltpu.VMEM((shards // 2, 2, count, features // 2), BF16),
+            pltpu.VMEM((groups, 2, count, features // 2), BF16),
+            pltpu.VMEM((2, count, features), BF16),
             sem((depth, 2 * members)),
             sem((2, count)),
             sem,
             sem((shards,)),
             sem((shards,)),
             sem((shards,)),
-            sem((shards,)),
+            sem((shards // groups,)),
             sem((groups,)),
             sem((groups,)),
-            sem((shards,)),
-            sem((shards,)),
-            sem((shards,)),
-            sem((shards,)),
-            sem((shards, chunks)),
-            sem((shards, chunks)),
+            sem((shards // 2,)),
+            sem((groups, shards // 2)),
+            sem((groups, shards // 2)),
+            sem((groups, shards)),
+            sem((chunks,)),
+            sem((chunks,)),
+            sem((shards // 2, chunks)),
+            sem((shards // 2, chunks)),
             sem((groups, chunks)),
             sem((groups, chunks)),
+            sem((chunks,)),
+            sem((chunks,)),
         ],
         compiler_params=pltpu.CompilerParams(
             collective_id=0, has_side_effects=True, vmem_limit_bytes=67043328

time: 70.3 us -> 69.5 us (0.989)
  Pallas kernels: 68.6 us -> 67.3 us
    pallas_call x1, Pallas kernels: 68.6 us -> 67.3 us  [on_device(): pl.pallas_call(functools.partial(layer_kernel, sizes), out_shape=jax.Shap...]
where the time goes in v2:
time: 69.5 us; the launch traced here: 68.8 us
  Pallas kernels  67.3 us (97%)
  local copies, waits for them, and re-layouts  1.47 us (2%)
    pallas_call x1, Pallas kernels, on_device(): pl.pallas_call(functools.partial(layer_kernel, sizes), out_shape=jax.Shap...  67.3 us
    unnamed x1, local copies, waits for them, and re-layouts  1.47 us

profile of v2, /device:TPU:0, one launch (start us, length us, event | category | flops | bytes accessed | tf_op | source)
XLA Modules:
  0.0 68.8 jit_solution(4332540760385054081)
XLA Ops:
  0.0 67.3 %layer.1 = bf16[8,4096]{1,0:T(8,128)(2,1)} custom-call(bf16[8,4096]{1,0:T(8,128)(2,1)} %hidden_ref.1, bf16[8,8,128]{2,1,0:T(8,128)(2,1)} %queries_ref.1, bf16[8,1024,128]{2,1,0:T(8,128)(2,1)} %bitcast.5, bf16[8,1024,128]{2,1,0:T(8,128)(2,1)} %bitcast.6, bf16[1024,512]{1,0:T(8,128)(2,1)} %out_weight_ref.1, bf16[32,128]{1,0:T(8,128)(2,1)} %bitcast.8, ...), custom_call_target="tpu_custom_call" | custom-call | tf_op jit(solution)/shard_map/layer/pallas_call | solution.py:482
  67.3 1.5 %copy.13 = bf16[8,4096]{1,0:T(8,128)(2,1)} copy(bf16[8,4096]{1,0:T(8,128)(2,1)} %layer.1) | data formatting | bytes 131072

commit v3 on v2

--- a/solution.py
+++ b/solution.py
@@ -411,12 +411,12 @@
         def _():
             down(t)
 
-        for lag, work in ((1, sum_cores), (2, sum_chips), (3, sum_groups)):
+        for lag, work in ((1, sum_cores), (4, sum_chips), (6, sum_groups)):
             @pl.when(jnp.logical_and(t >= lag, t < chunks + lag))
             def _():
                 work(t - lag)
 
-    each(chunks + 3, stage)
+    each(chunks + 6, stage)
     each(chunks, lambda c: final_copy(c, core).wait_recv())
     out_ref[...] = final[core]
 

time: 69.5 us -> 61.6 us (0.89)
  Pallas kernels: 67.3 us -> 59.3 us
    pallas_call x1, Pallas kernels: 67.3 us -> 59.3 us  [on_device(): pl.pallas_call(functools.partial(layer_kernel, sizes), out_shape=jax.Shap...]
where the time goes in v3:
time: 61.6 us; the launch traced here: 60.8 us
  Pallas kernels  59.3 us (96%)
  local copies, waits for them, and re-layouts  1.47 us (2%)
    pallas_call x1, Pallas kernels, on_device(): pl.pallas_call(functools.partial(layer_kernel, sizes), out_shape=jax.Shap...  59.3 us
    unnamed x1, local copies, waits for them, and re-layouts  1.47 us

profile of v3, /device:TPU:0, one launch (start us, length us, event | category | flops | bytes accessed | tf_op | source)
XLA Modules:
  0.0 60.8 jit_solution(15997718906222947886)
XLA Ops:
  0.0 59.3 %layer.1 = bf16[8,4096]{1,0:T(8,128)(2,1)} custom-call(bf16[8,4096]{1,0:T(8,128)(2,1)} %hidden_ref.1, bf16[8,8,128]{2,1,0:T(8,128)(2,1)} %queries_ref.1, bf16[8,1024,128]{2,1,0:T(8,128)(2,1)} %bitcast.5, bf16[8,1024,128]{2,1,0:T(8,128)(2,1)} %bitcast.6, bf16[1024,512]{1,0:T(8,128)(2,1)} %out_weight_ref.1, bf16[32,128]{1,0:T(8,128)(2,1)} %bitcast.8, ...), custom_call_target="tpu_custom_call" | custom-call | tf_op jit(solution)/shard_map/layer/pallas_call | solution.py:482
  59.4 1.5 %copy.13 = bf16[8,4096]{1,0:T(8,128)(2,1)} copy(bf16[8,4096]{1,0:T(8,128)(2,1)} %layer.1) | data formatting | bytes 131072
